TPU v7x, 512 devices: a whole 4x8x8 slice. The times are simulated.
512 devices in a mesh: req: 128 (over y, z, core), tp: 4 (over x).
Axes of the slice: x: 4, y: 8, z: 8, core: 2. Of those that a mesh axis runs over, the one named last changes fastest.
Arguments:
- hidden: bfloat16 [1024, 4096], P('req'), may hold values from -512 to 512
- norm_gain: bfloat16 [4096], replicated, may hold values from 1 to 3
- lm_head: bfloat16 [4096, 131072], P(None, ('req', 'tp'))
- targets: int32 [1024], P('req'), may hold values from 0 to 131071
- segments: int32 [1024], P('req'), may hold values from 0 to 3, never falling along the last dimension, each value on 1 to 512 neighbouring positions
- scored: int32 [1024], P('req'), may hold values from 0 to 1, as said below
Outputs:
- token_logprob: float32 [1024], P('req')
- token_entropy: float32 [1024], P('req')
- seq_logprob: float32 [4], replicated
Inputs may be any that keep to these rules, and one draw needn't show every extreme that they name: At most 4 of the 8 rows of one index of req are scored, and exactly 4 on some index in every draw.
All inputs are finite; a program needn't handle non-finite values.
Results may differ from a plain program's by a relative error of at most 0.0061.
Values may be sent and summed in bfloat16 or wider, within the bound.
A program may use at most 64 MiB of HBM per device.

v0:
```python
import jax
import jax.numpy as jnp
from jax import lax
from jax.sharding import PartitionSpec as P

SEQS = 4
SCORE_MOST = 4


def local(hidden, norm_gain, lm_head, targets, segments, scored):
    col_width = lm_head.shape[1]
    own_index = lax.axis_index("req")
    first_col = (own_index * lax.axis_size("tp") + lax.axis_index("tp")) * col_width
    rank = jnp.cumsum(scored) - 1
    slots = jnp.arange(SCORE_MOST, dtype=jnp.int32)
    chosen = (scored[None, :] == 1) & (rank[None, :] == slots[:, None])
    values = jnp.sum(
        jnp.where(chosen[:, :, None], hidden.astype(jnp.float32)[None, :, :], 0.0), axis=1
    )
    row_scale = lax.rsqrt(jnp.mean(values * values, axis=1, keepdims=True) + 1e-05)
    normed = (values * row_scale * norm_gain.astype(jnp.float32)[None, :]).astype(jnp.bfloat16)
    codes = jnp.sum(jnp.where(chosen, (targets * SEQS + segments + 1)[None, :], 0), axis=1) - 1
    rows, row_codes = lax.all_gather((normed, codes), "req", axis=0, tiled=True)
    used = row_codes >= 0
    row_targets = row_codes // SEQS
    row_segments = row_codes % SEQS
    logits = jnp.dot(rows, lm_head, preferred_element_type=jnp.float32)
    own_top = jnp.max(logits, axis=1)
    scaled = jnp.exp(logits - own_top[:, None])
    own_total = jnp.sum(scaled, axis=1)
    own_weighted = jnp.sum(scaled * logits, axis=1)
    columns = first_col + jnp.arange(col_width, dtype=jnp.int32)
    own_picked = jnp.sum(jnp.where(columns[None, :] == row_targets[:, None], logits, 0.0), axis=1)
    row_top = lax.pmax(own_top, ("req", "tp"))
    factor = jnp.exp(own_top - row_top)
    sums = lax.psum(
        jnp.stack([own_total * factor, own_weighted * factor, own_picked]), ("req", "tp")
    )
    log_norm = row_top + jnp.log(sums[0])
    logprob = jnp.where(used, sums[2] - log_norm, 0.0)
    entropy = jnp.where(used, log_norm - sums[1] / sums[0], 0.0)
    seq_ids = jnp.arange(SEQS, dtype=jnp.int32)
    seq_logprob = jnp.sum(
        jnp.where(row_segments[None, :] == seq_ids[:, None], logprob[None, :], 0.0), axis=1
    )
    own = own_index * SCORE_MOST
    own_logprob = lax.dynamic_slice_in_dim(logprob, own, SCORE_MOST, 0)
    own_entropy = lax.dynamic_slice_in_dim(entropy, own, SCORE_MOST, 0)
    token_logprob = jnp.sum(jnp.where(chosen, own_logprob[:, None], 0.0), axis=0)
    token_entropy = jnp.sum(jnp.where(chosen, own_entropy[:, None], 0.0), axis=0)
    return (token_logprob, token_entropy, seq_logprob)


def solution(mesh):
    return jax.shard_map(
        local,
        mesh=mesh,
        in_specs=(P("req", None), P(), P(None, ("req", "tp")), P("req"), P("req"), P("req")),
        out_specs=(P("req"), P("req"), P()),
        check_vma=False,
    )
```

profile of v0, /device:TPU:1, one launch (start us, length us, event | category | flops | bytes accessed | tf_op | source)
XLA Modules:
  0.0 312.4 jit_solution(14411869433341832396)
XLA Ops:
  7.2 0.0 all-gather.3.cloned.1.call-start
  7.2 0.8 broadcast_compare_fusion.2
  8.0 0.8 reduce-window.8
  8.9 0.8 convert_element_type.9
  9.7 0.7 add_add_fusion
  10.4 0.1 select_reduce_fusion.5
  10.5 0.2 select_reduce_fusion.1
  10.7 0.1 multiply_reduce_fusion.1
  10.9 0.7 convert_element_type.10
  11.6 0.7 fusion.1
  12.3 0.0 all-gather.3.cloned.1.call-update
  12.3 1.3 dynamic-slice
  14.3 0.1 add_dynamic-update-slice_fusion
  14.4 27.8 %all-reduce = s32[512]{0:T(512)S(1)} all-reduce(s32[512]{0:T(512)S(1)} %add_dynamic-update-slice_fusion), channel_id=1, replica_groups=mesh['req'=128,'tp'=4] {'req'}, use_global_device_ids=true, to_apply=%add | all-reduce | flops 512 | bytes 4096
  42.2 60.8 %all-gather.3.cloned.1.call-done = bf16[128,4,4096]{2,1,0:T(4,128)(2,1)} async-done(((bf16[1,4,4096]{2,1,0:T(4,128)(2,1)}), bf16[128,4,4096]{2,1,0:T(4,128)(2,1)}) %all-gather.3.cloned.1.call-update) | async-done | bytes 4194320 | tf_op jit(solution)/shard_map/all_gather | solution.py:23
  103.0 6.9 %reshape.92 = bf16[512,4096]{1,0:T(8,128)(2,1)} reshape(bf16[128,4,4096]{2,1,0:T(4,128)(2,1)} %all-gather.3.cloned.1.call-done) | data formatting | bytes 8388608
  109.9 3.5 %fusion.7 = (f32[512]{0:T(512)S(1)}, f32[512,256]{0,1:T(8,128)S(1)}) fusion(bf16[512,4096]{1,0:T(8,128)(2,1)} %reshape.92, bf16[4096,256]{1,0:T(8,128)(2,1)S(1)} %copy-done), kind=kOutput, calls=%fused_computation.38 | convolution fusion | flops 1073872384 | bytes 6817792 | tf_op jit(solution)/shard_map/dot_general | solution.py:27
  113.4 96.0 %pmax.7 = f32[512]{0:T(512)S(1)} all-reduce(f32[512]{0:T(512)S(1)} %get-tuple-element.19), channel_id=1, replica_groups=mesh['req'=128,'tp'=4] {'req','tp'}, use_global_device_ids=true, to_apply=%region_6.7 | all-reduce | flops 512 | bytes 4096 | tf_op jit(solution)/shard_map/pmax | solution.py:34
  209.5 0.2 fusion
  209.7 94.4 %psum.7 = f32[3,512]{1,0:T(4,128)S(1)} all-reduce(f32[3,512]{1,0:T(4,128)S(1)} %pad_maximum_fusion), channel_id=1, replica_groups=mesh['req'=128,'tp'=4] {'req','tp'}, use_global_device_ids=true, to_apply=%region_9.10 | all-reduce | flops 1536 | bytes 12288 | tf_op jit(solution)/shard_map/psum | solution.py:36
  304.1 0.6 select_reduce_fusion.2
  304.8 0.1 dynamic_slice.6
  304.8 0.1 dynamic_slice.7
  304.9 0.6 select_reduce_fusion.3
  (12 shorter events, 0.1 us)
Async XLA Ops:
  7.2 102.8 %copy-start = (bf16[4096,256]{1,0:T(8,128)(2,1)S(1)}, bf16[4096,256]{1,0:T(8,128)(2,1)}, u32[]{:S(2)}) copy-start(bf16[4096,256]{1,0:T(8,128)(2,1)} %param.8) | copy-start | bytes 6291460
  7.2 95.9 %all-gather.3.cloned.1.call-start = ((), (), s32[]{:S(2)}) async-start(), calls=%async_computation | async-start | bytes 4227072 | tf_op jit(solution)/shard_map/all_gather | solution.py:23
Sparse Core Ops, SparseCore 0:
  12.4 90.5 all-gather.2
where the time goes:
time: 313 us; the launch traced here: 312 us
  blocking collectives  218 us (70%)
  waiting for transfers between devices  60.9 us (19%)
  between operations  14.7 us (5%)
  local copies, waits for them, and re-layouts  8.34 us (3%)
  other arithmetic  6.62 us (2%)
  matrix products  3.49 us (1%)
    pmax x1, blocking collectives, local(): row_top = lax.pmax(own_top, ('req', 'tp'))  96 us
    psum x1, blocking collectives, local(): lax.psum(jnp.stack([own_total * factor, own_weighted * factor, own_picked...  94.4 us
    all_gather x1, waiting for transfers between devices, local(): rows, row_codes = lax.all_gather((normed, codes), 'req', axis=0, tiled=True)  60.8 us
    unnamed x1, blocking collectives  27.8 us
    unnamed x5, local copies, waits for them, and re-layouts  8.19 us
  transfers between devices with their start and end apart: 1, of which 1 were waited for; matrix products, arithmetic and copies ran while one was open for 0% of the time, Pallas kernels for 0%

commit v1 on v0

--- a/solution.py
+++ b/solution.py
@@ -34,7 +34,7 @@
     row_top = lax.pmax(own_top, ("req", "tp"))
     factor = jnp.exp(own_top - row_top)
     sums = lax.psum(
-        jnp.stack([own_total * factor, own_weighted * factor, own_picked]), ("req", "tp")
+        lax.psum(jnp.stack([own_total * factor, own_weighted * factor, own_picked]), "req"), "tp"
     )
     log_norm = row_top + jnp.log(sums[0])
     logprob = jnp.where(used, sums[2] - log_norm, 0.0)

time: 313 us -> 478 us (1.53)
  blocking collectives: 218 us -> 381 us
    psum x1, blocking collectives: 94.4 us -> 251 us  [local(): lax.psum(jnp.stack([own_total * factor, own_weighted * factor, own_picked...]
    psum x0 -> x1, blocking collectives: none -> 6.67 us  [local(): lax.psum(lax.psum(jnp.stack([own_total * factor, own_weighted * factor, o...]
where the time goes in v1:
time: 478 us; the launch traced here: 476 us
  blocking collectives  381 us (80%)
  waiting for transfers between devices  60.9 us (13%)
  between operations  14.8 us (3%)
  local copies, waits for them, and re-layouts  8.34 us (2%)
  other arithmetic  6.62 us (1%)
    psum x1, blocking collectives, local(): lax.psum(jnp.stack([own_total * factor, own_weighted * factor, own_picked...  251 us
    pmax x1, blocking collectives, local(): row_top = lax.pmax(own_top, ('req', 'tp'))  96 us
    all_gather x1, waiting for transfers between devices, local(): rows, row_codes = lax.all_gather((normed, codes), 'req', axis=0, tiled=True)  60.8 us
    unnamed x1, blocking collectives  27.8 us
  transfers between devices with their start and end apart: 1, of which 1 were waited for; matrix products, arithmetic and copies ran while one was open for 0% of the time, Pallas kernels for 0%

profile of v1, /device:TPU:1, one launch (start us, length us, event | category | flops | bytes accessed | tf_op | source)
XLA Modules:
  0.0 475.5 jit_solution(8155348628457912142)
XLA Ops:
  7.2 0.0 all-gather.3.cloned.1.call-start
  7.2 0.8 broadcast_compare_fusion.2
  8.0 0.8 reduce-window.8
  8.9 0.8 convert_element_type.9
  9.7 0.7 add_add_fusion
  10.4 0.1 select_reduce_fusion.5
  10.5 0.2 select_reduce_fusion.1
  10.7 0.1 multiply_reduce_fusion.1
  10.9 0.7 convert_element_type.10
  11.6 0.7 fusion.1
  12.3 1.3 dynamic-slice
  14.3 0.1 add_dynamic-update-slice_fusion
  14.4 27.8 %all-reduce = s32[512]{0:T(512)S(1)} all-reduce(s32[512]{0:T(512)S(1)} %add_dynamic-update-slice_fusion), channel_id=1, replica_groups=mesh['req'=128,'tp'=4] {'req'}, use_global_device_ids=true, to_apply=%add | all-reduce | flops 512 | bytes 4096
  42.2 60.8 %all-gather.3.cloned.1.call-done = bf16[128,4,4096]{2,1,0:T(4,128)(2,1)} async-done(((bf16[1,4,4096]{2,1,0:T(4,128)(2,1)}), bf16[128,4,4096]{2,1,0:T(4,128)(2,1)}) %all-gather.3.cloned.1.call-update) | async-done | bytes 4194320 | tf_op jit(solution)/shard_map/all_gather | solution.py:23
  103.0 6.9 %reshape.92 = bf16[512,4096]{1,0:T(8,128)(2,1)} reshape(bf16[128,4,4096]{2,1,0:T(4,128)(2,1)} %all-gather.3.cloned.1.call-done) | data formatting | bytes 8388608
  109.9 3.5 fusion.7
  113.4 96.0 %pmax.7 = f32[512]{0:T(512)S(1)} all-reduce(f32[512]{0:T(512)S(1)} %get-tuple-element.19), channel_id=1, replica_groups=mesh['req'=128,'tp'=4] {'req','tp'}, use_global_device_ids=true, to_apply=%region_6.7 | all-reduce | flops 512 | bytes 4096 | tf_op jit(solution)/shard_map/pmax | solution.py:34
  209.5 0.2 fusion
  209.7 250.9 %psum.14 = f32[3,512]{1,0:T(4,128)S(1)} all-reduce(f32[3,512]{1,0:T(4,128)S(1)} %pad_maximum_fusion), channel_id=1, replica_groups=mesh['req'=128,'tp'=4] {'req'}, use_global_device_ids=true, to_apply=%region_9.10 | all-reduce | flops 1536 | bytes 12288 | tf_op jit(solution)/shard_map/psum | solution.py:37
  460.6 6.7 %psum.15 = f32[3,512]{1,0:T(4,128)S(1)} all-reduce(f32[3,512]{1,0:T(4,128)S(1)} %psum.14), channel_id=1, replica_groups=mesh['req'=128,'tp'=4] {'tp'}, use_global_device_ids=true, to_apply=%region_10.11 | all-reduce | flops 1536 | bytes 12288 | tf_op jit(solution)/shard_map/psum | solution.py:36
  467.3 0.6 select_reduce_fusion.2
  467.9 0.1 dynamic_slice.6
  468.0 0.1 dynamic_slice.7
  468.1 0.6 select_reduce_fusion.3
  (13 shorter events, 0.1 us)
Async XLA Ops:
  7.2 102.8 %copy-start = (bf16[4096,256]{1,0:T(8,128)(2,1)S(1)}, bf16[4096,256]{1,0:T(8,128)(2,1)}, u32[]{:S(2)}) copy-start(bf16[4096,256]{1,0:T(8,128)(2,1)} %param.8) | copy-start | bytes 6291460
  7.2 95.9 %all-gather.3.cloned.1.call-start = ((), (), s32[]{:S(2)}) async-start(), calls=%async_computation | async-start | bytes 4227072 | tf_op jit(solution)/shard_map/all_gather | solution.py:23
Sparse Core Ops, SparseCore 0:
  12.4 90.5 all-gather.2

commit v2 on v0

--- a/solution.py
+++ b/solution.py
@@ -33,8 +33,11 @@
     own_picked = jnp.sum(jnp.where(columns[None, :] == row_targets[:, None], logits, 0.0), axis=1)
     row_top = lax.pmax(own_top, ("req", "tp"))
     factor = jnp.exp(own_top - row_top)
-    sums = lax.psum(
-        jnp.stack([own_total * factor, own_weighted * factor, own_picked]), ("req", "tp")
+    sums = jnp.sum(
+        lax.all_gather(
+            jnp.stack([own_total * factor, own_weighted * factor, own_picked]), ("req", "tp")
+        ),
+        axis=0,
     )
     log_norm = row_top + jnp.log(sums[0])
     logprob = jnp.where(used, sums[2] - log_norm, 0.0)

time: 313 us -> 336 us (1.073)
  waiting for transfers between devices: 60.9 us -> 175 us
  blocking collectives: 218 us -> 124 us
  other arithmetic: 6.62 us -> 10 us
    all_gather x0 -> x1, waiting for transfers between devices: none -> 114 us  [local(): lax.all_gather(jnp.stack([own_total * factor, own_weighted * factor, own_...]
    psum x1 -> x0, blocking collectives: 94.4 us -> none  [local(): lax.psum(jnp.stack([own_total * factor, own_weighted * factor, own_picked...]
  transfers between devices with their start and end apart: 1 -> 2, of which waited for: 1 -> 2; matrix products, arithmetic and copies ran while one was open for 0% -> 0% of each run, Pallas kernels for 0% -> 0%
where the time goes in v2:
time: 336 us; the launch traced here: 335 us
  waiting for transfers between devices  175 us (52%)
  blocking collectives  124 us (37%)
  between operations  14.8 us (4%)
  other arithmetic  10 us (3%)
  local copies, waits for them, and re-layouts  8.34 us (2%)
  matrix products  3.49 us (1%)
    all_gather x1, waiting for transfers between devices, local(): lax.all_gather(jnp.stack([own_total * factor, own_weighted * factor, own_...  114 us
    pmax x1, blocking collectives, local(): row_top = lax.pmax(own_top, ('req', 'tp'))  96 us
    all_gather x1, waiting for transfers between devices, local(): rows, row_codes = lax.all_gather((normed, codes), 'req', axis=0, tiled=True)  60.8 us
    unnamed x1, blocking collectives  27.8 us
    unnamed x5, local copies, waits for them, and re-layouts  8.19 us
  transfers between devices with their start and end apart: 2, of which 2 were waited for; matrix products, arithmetic and copies ran while one was open for 0% of the time, Pallas kernels for 0%

profile of v2, /device:TPU:1, one launch (start us, length us, event | category | flops | bytes accessed | tf_op | source)
XLA Modules:
  0.0 335.3 jit_solution(6106553528553639565)
XLA Ops:
  7.2 0.8 broadcast_compare_fusion.2
  8.0 0.8 reduce-window.8
  8.9 0.8 convert_element_type.9
  9.7 0.7 add_add_fusion
  10.4 0.1 select_reduce_fusion.5
  10.5 0.2 select_reduce_fusion.1
  10.7 0.1 multiply_reduce_fusion.1
  10.9 0.7 convert_element_type.10
  11.6 0.7 fusion.1
  12.4 1.3 dynamic-slice
  14.3 0.1 add_dynamic-update-slice_fusion
  14.4 27.8 %all-reduce = s32[512]{0:T(512)S(1)} all-reduce(s32[512]{0:T(512)S(1)} %add_dynamic-update-slice_fusion), channel_id=1, replica_groups=mesh['req'=128,'tp'=4] {'req'}, use_global_device_ids=true, to_apply=%add | all-reduce | flops 512 | bytes 4096
  42.3 60.8 %all-gather.6.cloned.1.call-done = bf16[128,4,4096]{2,1,0:T(4,128)(2,1)} async-done(((bf16[1,4,4096]{2,1,0:T(4,128)(2,1)}), bf16[128,4,4096]{2,1,0:T(4,128)(2,1)}) %all-gather.6.cloned.1.call-update) | async-done | bytes 4194320 | tf_op jit(solution)/shard_map/all_gather | solution.py:23
  103.0 6.9 %reshape.93 = bf16[512,4096]{1,0:T(8,128)(2,1)} reshape(bf16[128,4,4096]{2,1,0:T(4,128)(2,1)} %all-gather.6.cloned.1.call-done) | data formatting | bytes 8388608
  109.9 3.5 %fusion.7 = (f32[512]{0:T(512)S(1)}, f32[512,256]{0,1:T(8,128)S(1)}) fusion(bf16[512,4096]{1,0:T(8,128)(2,1)} %reshape.93, bf16[4096,256]{1,0:T(8,128)(2,1)S(1)} %copy-done), kind=kOutput, calls=%fused_computation.38 | convolution fusion | flops 1073872384 | bytes 6817792 | tf_op jit(solution)/shard_map/dot_general | solution.py:27
  113.4 96.0 %pmax.7 = f32[512]{0:T(512)S(1)} all-reduce(f32[512]{0:T(512)S(1)} %get-tuple-element.19), channel_id=1, replica_groups=mesh['req'=128,'tp'=4] {'req','tp'}, use_global_device_ids=true, to_apply=%region_6.7 | all-reduce | flops 512 | bytes 4096 | tf_op jit(solution)/shard_map/pmax | solution.py:34
  209.5 0.2 fusion
  209.7 0.6 maximum_bitcast_fusion
  210.3 113.9 %all-gather.8.cloned.1.call-done = f32[512,3,512]{2,1,0:T(4,128)} async-done(((f32[1,3,512]{2,1,0:T(4,128)}), f32[512,3,512]{2,1,0:T(4,128)}) %all-gather.8.cloned.1.call-update) | async-done | bytes 3145744 | tf_op jit(solution)/shard_map/all_gather | solution.py:37
  324.2 2.8 reduce_sum.96
  327.1 0.6 select_reduce_fusion.2
  327.7 0.1 dynamic_slice.6
  327.8 0.1 dynamic_slice.7
  327.8 0.6 select_reduce_fusion.3
  (15 shorter events, 0.2 us)
Async XLA Ops:
  7.2 102.8 %copy-start = (bf16[4096,256]{1,0:T(8,128)(2,1)S(1)}, bf16[4096,256]{1,0:T(8,128)(2,1)}, u32[]{:S(2)}) copy-start(bf16[4096,256]{1,0:T(8,128)(2,1)} %param.8) | copy-start | bytes 6291460
  7.2 95.9 %all-gather.6.cloned.1.call-start = ((), (), s32[]{:S(2)}) async-start(), calls=%async_computation | async-start | bytes 4227072 | tf_op jit(solution)/shard_map/all_gather | solution.py:23
  12.3 311.9 %all-gather.8.cloned.1.call-start = ((), (), s32[]{:S(2)}) async-start(), calls=%async_computation.1 | async-start | bytes 4202496 | tf_op jit(solution)/shard_map/all_gather | solution.py:37
Sparse Core Ops, SparseCore 0:
  12.4 90.5 all-gather.5
  210.4 113.7 all-gather.7
